TPU v7x, 128 devices: a whole 4x4x4 slice. The times are simulated.
128 devices in a mesh: replica: 16 (over z_lo, x, core), shard: 8 (over y, z_hi).
Axes of the slice: x: 4, y: 4, z: 4 (z_hi: 2, z_lo: 2; z = z_hi * 2 + z_lo), core: 2. Of those that a mesh axis runs over, the one named last changes fastest.
Arguments:
- params: float32 [16, 128, 28672], P('replica', 'shard'), may hold values from -6 to 6
- first_moment: float32 [16, 128, 28672], P('replica', 'shard'), may hold values from -3 to 3
- second_moment: float32 [16, 128, 28672], P('replica', 'shard'), may hold values from 0.25 to 4
- grads: bfloat16 [4, 16, 128, 28672], P(None, 'replica', 'shard'), may hold values from -6 to 6
- push_weight: float32 [16], P('replica'), may hold values from 0.5 to 2
Outputs:
- final_weights: bfloat16 [16, 128, 28672], P('replica')
All inputs are finite; a program needn't handle non-finite values.
Results may differ from a plain program's by a relative error of at most 0.001.
Values may be sent and summed in bfloat16 or wider, within the bound.
No kernel may reach another device: no remote copies, remote signals or barrier semaphores. Data moves between devices by JAX's collectives and lax.ppermute only.
A program may use at most 64 MiB of HBM per device.

v0:
```python
import jax
import jax.numpy as jnp
from jax import lax
from jax.sharding import PartitionSpec as P

STEPS = 4
beta_one = 0.9
beta_two = 0.95
learn_rate = 0.1
decay_rate = 0.1
epsilon = 1e-08
adam_offset = 101


def passed_along(value, axis, steps):
    count = lax.axis_size(axis)
    pairs = [(source, (source + steps) % count) for source in range(count)]
    return lax.ppermute(value, axis, pairs)


def adam_block(numer, first_moment, second_moment, gradient, weight, first_fix, second_fix):
    scale = weight[:, None, None]
    current = numer / scale
    gradient = gradient.astype(jnp.float32)
    first_moment = beta_one * first_moment + (1.0 - beta_one) * gradient
    second_moment = beta_two * second_moment + (1.0 - beta_two) * gradient * gradient
    update = first_moment / first_fix / (jnp.sqrt(second_moment / second_fix) + epsilon)
    current = current - learn_rate * (update + decay_rate * current)
    return (current * scale, first_moment, second_moment)


def per_device(params, first_moment, second_moment, grads, push_weight):
    replicas = lax.axis_size("replica")
    levels = replicas.bit_length() - 1
    weight = push_weight
    numer = params * weight[:, None, None]
    for iteration in range(STEPS):
        distance = 2 ** (iteration % levels)
        count = adam_offset + iteration
        first_fix = 1.0 - beta_one**count
        second_fix = 1.0 - beta_two**count
        gradient = grads[iteration]
        numer, first_moment, second_moment = adam_block(
            numer, first_moment, second_moment, gradient, weight, first_fix, second_fix
        )
        arrived, arrived_weight = passed_along((numer, weight), "replica", distance)
        numer = 0.5 * numer + 0.5 * arrived
        weight = 0.5 * weight + 0.5 * arrived_weight
    result = (numer / weight[:, None, None]).astype(jnp.bfloat16)
    return lax.all_gather(result, "shard", axis=1, tiled=True)


def solution(mesh):
    return jax.shard_map(
        per_device,
        mesh=mesh,
        in_specs=(
            P("replica", "shard", None),
            P("replica", "shard", None),
            P("replica", "shard", None),
            P(None, "replica", "shard", None),
            P("replica"),
        ),
        out_specs=P("replica", None, None),
        check_vma=False,
    )
```

profile of v0, /device:TPU:1, one launch (start us, length us, event | category | flops | bytes accessed | tf_op | source)
XLA Modules:
  0.0 283.7 jit_solution(8978683002006352249)
XLA Ops:
  6.5 0.0 all-gather.2.cloned.1.call-start
  7.2 0.0 copy-start
  7.2 0.0 copy-start.1
  7.2 0.0 copy-start.2
  7.2 4.6 %subtract_multiply_fusion.2 = f32[1,16,28672]{2,1,0:T(8,128)S(1)} fusion(f32[1,16,28672]{2,1,0:T(8,128)} %param.5, f32[1,16,28672]{2,1,0:T(8,128)} %param.6, f32[1,16,28672]{2,1,0:T(8,128)} %param.7, f32[]{:T(128)} %bitcast.45, bf16[4,1,16,28672]{3,2,1,0:T(8,128)(2,1)} %param.8), kind=kLoop, calls=%fused_computation.32 | loop fusion | flops 8716288 | bytes 8257540 | tf_op jit(solution)/shard_map/mul | solution.py:29
  11.8 2.7 collective-permute-start
  14.5 0.1 collective-permute-start.1
  14.6 20.1 %collective-permute-done.1 = f32[1]{0:T(128)} collective-permute-done((f32[1]{0:T(128)}, f32[1]{0:T(128)}, u32[]{:S(2)}, u32[]{:S(2)}) %collective-permute-start.1) | collective-permute-done | bytes 36 | tf_op jit(solution)/shard_map/ppermute | solution.py:18
  35.2 0.0 collective-permute-done
  35.3 0.0 copy-done
  35.3 0.0 copy-done.1
  35.3 0.0 copy-done.2
  35.3 2.2 subtract_multiply_fusion.1
  37.5 1.3 collective-permute-start.2
  38.8 37.3 %collective-permute-start.3 = (f32[1]{0:T(128)}, f32[1]{0:T(128)}, u32[]{:S(2)}, u32[]{:S(2)}) collective-permute-start(f32[1]{0:T(128)} %add.83), channel_id=1, source_target_pairs={{0,16},{8,24},{16,32},{24,40},{32,48},{40,56},{48,64},{56,72},{64,... | collective-permute-start | bytes 20 | tf_op jit(solution)/shard_map/ppermute | solution.py:18
  76.1 1.6 collective-permute-done.3
  78.2 0.0 collective-permute-done.2
  78.2 2.7 subtract_multiply_fusion
  80.9 2.2 collective-permute-start.4
  83.1 36.5 %collective-permute-start.5 = (f32[1]{0:T(128)}, f32[1]{0:T(128)}, u32[]{:S(2)}, u32[]{:S(2)}) collective-permute-start(f32[1]{0:T(128)} %add.89), channel_id=1, source_target_pairs={{0,32},{8,40},{16,48},{24,56},{32,64},{40,72},{48,80},{56,88},{64,... | collective-permute-start | bytes 20 | tf_op jit(solution)/shard_map/ppermute | solution.py:18
  119.6 0.7 collective-permute-done.5
  120.8 0.0 collective-permute-done.4
  120.8 3.1 %fusion.12 = f32[1,16,28672]{2,1,0:T(8,128)S(1)} fusion(f32[1,16,28672]{2,1,0:T(8,128)S(1)} %subtract_multiply_fusion, f32[1,16,28672]{2,1,0:T(8,128)S(1)} %collective-permute-done.4, bf16[4,1,16,28672]{3,2,1,0:T(8,128)(2,1)S(1)} %copy-done.2, f32[]{:T(128)} %bitcast.9, f32[1,16,28672]{2,1,0:T(8,128)S(1)} %copy-done, f32[1,16,28672]{2,1,0:T(8,128)S(1)} %copy-done.1), kind=kLoop, calls=%fused_computation.24 | loop fusion | flops 20185088 | bytes 12845060 | tf_op jit(solution)/shard_map/mul | solution.py:29
  124.0 1.6 collective-permute-start.6
  125.5 33.5 %collective-permute-start.7 = (f32[1]{0:T(128)}, f32[1]{0:T(128)}, u32[]{:S(2)}, u32[]{:S(2)}) collective-permute-start(f32[1]{0:T(128)} %add.95), channel_id=1, source_target_pairs={{0,64},{8,72},{16,80},{24,88},{32,96},{40,104},{48,112},{56,120},{... | collective-permute-start | bytes 20 | tf_op jit(solution)/shard_map/ppermute | solution.py:18
  159.1 0.8 collective-permute-done.7
  160.4 0.0 collective-permute-done.6
  160.4 1.2 divide_convert_fusion
  161.7 0.0 all-gather.2.cloned.1.call-update
  161.7 108.4 %all-gather.2.cloned.1.call-done = bf16[1,128,28672]{2,1,0:T(8,128)(2,1)} async-done(((bf16[1,16,28672]{2,1,0:T(8,128)(2,1)}), bf16[1,128,28672]{2,1,0:T(8,128)(2,1)}) %all-gather.2.cloned.1.call-update) | async-done | bytes 7340048 | tf_op jit(solution)/shard_map/all_gather | solution.py:50
  270.1 6.8 %copy.8 = bf16[1,128,28672]{2,1,0:T(8,128)(2,1)} copy(bf16[1,128,28672]{2,1,0:T(8,128)(2,1)} %all-gather.2.cloned.1.call-done) | data formatting | bytes 14680064
Async XLA Ops:
  6.5 263.5 %all-gather.2.cloned.1.call-start = ((), (), s32[]{:S(2)}) async-start(), calls=%async_computation | async-start | bytes 8257536 | tf_op jit(solution)/shard_map/all_gather | solution.py:50
  7.2 28.1 %copy-start = (f32[1,16,28672]{2,1,0:T(8,128)S(1)}, f32[1,16,28672]{2,1,0:T(8,128)}, u32[]{:S(2)}) copy-start(f32[1,16,28672]{2,1,0:T(8,128)} %param.6) | copy-start | bytes 5505028
  7.2 28.1 %copy-start.1 = (f32[1,16,28672]{2,1,0:T(8,128)S(1)}, f32[1,16,28672]{2,1,0:T(8,128)}, u32[]{:S(2)}) copy-start(f32[1,16,28672]{2,1,0:T(8,128)} %param.7) | copy-start | bytes 5505028
  7.2 28.1 %copy-start.2 = (bf16[4,1,16,28672]{3,2,1,0:T(8,128)(2,1)S(1)}, bf16[4,1,16,28672]{3,2,1,0:T(8,128)(2,1)}, u32[]{:S(2)}) copy-start(bf16[4,1,16,28672]{3,2,1,0:T(8,128)(2,1)} %param.8) | copy-start | bytes 11010052
  11.8 23.4 %collective-permute-start = (f32[1,16,28672]{2,1,0:T(8,128)S(1)}, f32[1,16,28672]{2,1,0:T(8,128)S(1)}, u32[]{:S(2)}, u32[]{:S(2)}) collective-permute-start(f32[1,16,28672]{2,1,0:T(8,128)S(1)} %subtract_multiply_fusion.2), channel_id=1, source_target_pairs={{0,8},{8,16},{16,24},{24,32},{32,40},{40,48},{48,56},{56,64},{64,7... | collective-permute-start | bytes 5505032 | tf_op jit(solution)/shard_map/ppermute | solution.py:18
  14.5 20.2 %collective-permute-start.1 = (f32[1]{0:T(128)}, f32[1]{0:T(128)}, u32[]{:S(2)}, u32[]{:S(2)}) collective-permute-start(f32[1]{0:T(128)} %param.9), channel_id=1, source_target_pairs={{0,8},{8,16},{16,24},{24,32},{32,40},{40,48},{48,56},{56,64},{64,7... | collective-permute-start | bytes 20 | tf_op jit(solution)/shard_map/ppermute | solution.py:18
  37.5 40.7 %collective-permute-start.2 = (f32[1,16,28672]{2,1,0:T(8,128)S(1)}, f32[1,16,28672]{2,1,0:T(8,128)S(1)}, u32[]{:S(2)}, u32[]{:S(2)}) collective-permute-start(f32[1,16,28672]{2,1,0:T(8,128)S(1)} %subtract_multiply_fusion.1), channel_id=1, source_target_pairs={{0,16},{8,24},{16,32},{24,40},{32,48},{40,56},{48,64},{56,72},{64,... | collective-permute-start | bytes 5505032 | tf_op jit(solution)/shard_map/ppermute | solution.py:18
  38.8 38.9 %collective-permute-start.3 = (f32[1]{0:T(128)}, f32[1]{0:T(128)}, u32[]{:S(2)}, u32[]{:S(2)}) collective-permute-start(f32[1]{0:T(128)} %add.83), channel_id=1, source_target_pairs={{0,16},{8,24},{16,32},{24,40},{32,48},{40,56},{48,64},{56,72},{64,... | collective-permute-start | bytes 20 | tf_op jit(solution)/shard_map/ppermute | solution.py:18
  80.9 39.9 %collective-permute-start.4 = (f32[1,16,28672]{2,1,0:T(8,128)S(1)}, f32[1,16,28672]{2,1,0:T(8,128)S(1)}, u32[]{:S(2)}, u32[]{:S(2)}) collective-permute-start(f32[1,16,28672]{2,1,0:T(8,128)S(1)} %subtract_multiply_fusion), channel_id=1, source_target_pairs={{0,32},{8,40},{16,48},{24,56},{32,64},{40,72},{48,80},{56,88},{64,... | collective-permute-start | bytes 5505032 | tf_op jit(solution)/shard_map/ppermute | solution.py:18
  83.1 37.2 %collective-permute-start.5 = (f32[1]{0:T(128)}, f32[1]{0:T(128)}, u32[]{:S(2)}, u32[]{:S(2)}) collective-permute-start(f32[1]{0:T(128)} %add.89), channel_id=1, source_target_pairs={{0,32},{8,40},{16,48},{24,56},{32,64},{40,72},{48,80},{56,88},{64,... | collective-permute-start | bytes 20 | tf_op jit(solution)/shard_map/ppermute | solution.py:18
  124.0 36.4 %collective-permute-start.6 = (f32[1,16,28672]{2,1,0:T(8,128)S(1)}, f32[1,16,28672]{2,1,0:T(8,128)S(1)}, u32[]{:S(2)}, u32[]{:S(2)}) collective-permute-start(f32[1,16,28672]{2,1,0:T(8,128)S(1)} %fusion.12), channel_id=1, source_target_pairs={{0,64},{8,72},{16,80},{24,88},{32,96},{40,104},{48,112},{56,120},{... | collective-permute-start | bytes 5505032 | tf_op jit(solution)/shard_map/ppermute | solution.py:18
  125.5 34.3 %collective-permute-start.7 = (f32[1]{0:T(128)}, f32[1]{0:T(128)}, u32[]{:S(2)}, u32[]{:S(2)}) collective-permute-start(f32[1]{0:T(128)} %add.95), channel_id=1, source_target_pairs={{0,64},{8,72},{16,80},{24,88},{32,96},{40,104},{48,112},{56,120},{... | collective-permute-start | bytes 20 | tf_op jit(solution)/shard_map/ppermute | solution.py:18
Sparse Core Ops, SparseCore 0:
  161.8 108.2 all-gather.1
where the time goes:
time: 284 us
  waiting for transfers between devices  132 us (46%)
  starting transfers between devices  115 us (40%)
  between operations  16.4 us (6%)
  other arithmetic  13.8 us (5%)
  local copies, waits for them, and re-layouts  6.79 us (2%)
    ppermute x8, starting transfers between devices, passed_along(): return lax.ppermute(value, axis, pairs)  115 us
    all_gather x1, waiting for transfers between devices, per_device(): return lax.all_gather(result, 'shard', axis=1, tiled=True)  108 us
    ppermute x8, waiting for transfers between devices, passed_along(): return lax.ppermute(value, axis, pairs)  23.2 us
    mul x4, other arithmetic, adam_block(): return (current * scale, first_moment, second_moment)  12.6 us
    unnamed x7, local copies, waits for them, and re-layouts  6.79 us
  transfers between devices with their start and end apart: 9, of which 5 were waited for; matrix products, arithmetic and copies ran while one was open for 0% of the time, Pallas kernels for 0%

commit v1 on v0

--- a/solution.py
+++ b/solution.py
@@ -47,7 +47,9 @@
         numer = 0.5 * numer + 0.5 * arrived
         weight = 0.5 * weight + 0.5 * arrived_weight
     result = (numer / weight[:, None, None]).astype(jnp.bfloat16)
-    return lax.all_gather(result, "shard", axis=1, tiled=True)
+    return jnp.concatenate(
+        lax.all_to_all(jnp.stack([result] * lax.axis_size("shard")), "shard", 0, 0), axis=1
+    )
 
 
 def solution(mesh):

time: 284 us -> 253 us (0.89)
  the two profiles are of different devices: /device:TPU:1 before, /device:TPU:6 now
where the time goes in v1:
time: 253 us
  starting transfers between devices  119 us (47%)
  blocking collectives  87.5 us (35%)
  waiting for transfers between devices  27 us (11%)
  other arithmetic  12.9 us (5%)
  local copies, waits for them, and re-layouts  3.76 us (1%)
  between operations  3.35 us (1%)
    ppermute x8, starting transfers between devices, passed_along(): return lax.ppermute(value, axis, pairs)  119 us
    all_to_all x1, blocking collectives, per_device(): lax.all_to_all(jnp.stack([result] * lax.axis_size('shard')), 'shard', 0, 0)  87.5 us
    ppermute x8, waiting for transfers between devices, passed_along(): return lax.ppermute(value, axis, pairs)  27 us
    mul x4, other arithmetic, adam_block(): return (current * scale, first_moment, second_moment)  12.6 us
  transfers between devices with their start and end apart: 8, of which 4 were waited for; matrix products, arithmetic and copies ran while one was open for 0% of the time, Pallas kernels for 0%

profile of v1, /device:TPU:6, one launch (start us, length us, event | category | flops | bytes accessed | tf_op | source)
XLA Modules:
  0.0 253.2 jit_solution(15310507040063948955)
XLA Ops:
  0.7 0.0 copy-start
  0.7 0.0 copy-start.1
  0.7 0.0 copy-start.2
  0.7 4.6 %subtract_multiply_fusion.2 = f32[1,16,28672]{2,1,0:T(8,128)S(1)} fusion(f32[1,16,28672]{2,1,0:T(8,128)} %param.5, f32[1,16,28672]{2,1,0:T(8,128)} %param.6, f32[1,16,28672]{2,1,0:T(8,128)} %param.7, f32[]{:T(128)} %bitcast.48, bf16[4,1,16,28672]{3,2,1,0:T(8,128)(2,1)} %param.8), kind=kLoop, calls=%fused_computation.32 | loop fusion | flops 8716288 | bytes 8257540 | tf_op jit(solution)/shard_map/mul | solution.py:29
  5.3 0.1 collective-permute-start
  5.3 1.9 collective-permute-start.1
  7.3 20.9 %collective-permute-done.1 = f32[1]{0:T(128)} collective-permute-done((f32[1]{0:T(128)}, f32[1]{0:T(128)}, u32[]{:S(2)}, u32[]{:S(2)}) %collective-permute-start.1) | collective-permute-done | bytes 36 | tf_op jit(solution)/shard_map/ppermute | solution.py:18
  28.8 0.0 collective-permute-done
  28.8 0.0 copy-done
  28.8 0.0 copy-done.1
  28.8 0.0 copy-done.2
  28.8 2.2 subtract_multiply_fusion.1
  31.1 4.0 %collective-permute-start.2 = (f32[1,16,28672]{2,1,0:T(8,128)S(1)}, f32[1,16,28672]{2,1,0:T(8,128)S(1)}, u32[]{:S(2)}, u32[]{:S(2)}) collective-permute-start(f32[1,16,28672]{2,1,0:T(8,128)S(1)} %subtract_multiply_fusion.1), channel_id=1, source_target_pairs={{0,16},{8,24},{16,32},{24,40},{32,48},{40,56},{48,64},{56,72},{64,... | collective-permute-start | bytes 5505032 | tf_op jit(solution)/shard_map/ppermute | solution.py:18
  35.1 36.4 %collective-permute-start.3 = (f32[1]{0:T(128)}, f32[1]{0:T(128)}, u32[]{:S(2)}, u32[]{:S(2)}) collective-permute-start(f32[1]{0:T(128)} %add.83), channel_id=1, source_target_pairs={{0,16},{8,24},{16,32},{24,40},{32,48},{40,56},{48,64},{56,72},{64,... | collective-permute-start | bytes 20 | tf_op jit(solution)/shard_map/ppermute | solution.py:18
  71.4 1.1 collective-permute-done.3
  73.2 0.0 collective-permute-done.2
  73.2 2.7 %subtract_multiply_fusion = f32[1,16,28672]{2,1,0:T(8,128)S(1)} fusion(f32[1,16,28672]{2,1,0:T(8,128)S(1)} %subtract_multiply_fusion.1, f32[1,16,28672]{2,1,0:T(8,128)S(1)} %collective-permute-done.2, f32[]{:T(128)} %bitcast.6, bf16[4,1,16,28672]{3,2,1,0:T(8,128)(2,1)S(1)} %copy-done.2, f32[1,16,28672]{2,1,0:T(8,128)S(1)} %copy-done, ...), kind=kLoop, calls=%fused_computation.30 | loop fusion | flops 16515072 | bytes 11927556 | tf_op jit(solution)/shard_map/mul | solution.py:29
  75.9 2.5 collective-permute-start.4
  78.4 36.8 %collective-permute-start.5 = (f32[1]{0:T(128)}, f32[1]{0:T(128)}, u32[]{:S(2)}, u32[]{:S(2)}) collective-permute-start(f32[1]{0:T(128)} %add.89), channel_id=1, source_target_pairs={{0,32},{8,40},{16,48},{24,56},{32,64},{40,72},{48,80},{56,88},{64,... | collective-permute-start | bytes 20 | tf_op jit(solution)/shard_map/ppermute | solution.py:18
  115.1 2.7 %collective-permute-done.5 = f32[1]{0:T(128)} collective-permute-done((f32[1]{0:T(128)}, f32[1]{0:T(128)}, u32[]{:S(2)}, u32[]{:S(2)}) %collective-permute-start.5) | collective-permute-done | bytes 36 | tf_op jit(solution)/shard_map/ppermute | solution.py:18
  118.4 0.0 collective-permute-done.4
  118.4 3.1 %fusion.12 = f32[1,16,28672]{2,1,0:T(8,128)S(1)} fusion(f32[1,16,28672]{2,1,0:T(8,128)S(1)} %subtract_multiply_fusion, f32[1,16,28672]{2,1,0:T(8,128)S(1)} %collective-permute-done.4, bf16[4,1,16,28672]{3,2,1,0:T(8,128)(2,1)S(1)} %copy-done.2, f32[]{:T(128)} %bitcast.9, f32[1,16,28672]{2,1,0:T(8,128)S(1)} %copy-done, f32[1,16,28672]{2,1,0:T(8,128)S(1)} %copy-done.1), kind=kLoop, calls=%fused_computation.24 | loop fusion | flops 20185088 | bytes 12845060 | tf_op jit(solution)/shard_map/mul | solution.py:29
  121.6 0.1 collective-permute-start.6
  121.7 36.9 %collective-permute-start.7 = (f32[1]{0:T(128)}, f32[1]{0:T(128)}, u32[]{:S(2)}, u32[]{:S(2)}) collective-permute-start(f32[1]{0:T(128)} %add.95), channel_id=1, source_target_pairs={{0,64},{8,72},{16,80},{24,88},{32,96},{40,104},{48,112},{56,120},{... | collective-permute-start | bytes 20 | tf_op jit(solution)/shard_map/ppermute | solution.py:18
  158.6 2.3 collective-permute-done.7
  161.5 0.0 collective-permute-done.6
  161.6 0.3 fusion.17
  161.9 0.7 stack.2
  162.6 87.5 %all_to_all.5 = bf16[8,1,16,28672]{3,2,1,0:T(8,128)(2,1)S(1)} all-to-all(bf16[8,1,16,28672]{3,2,1,0:T(8,128)(2,1)S(1)} %stack.2), channel_id=1, replica_groups=mesh['replica'=16,'shard'=8] {'shard'}, dimensions={0} | all-to-all | bytes 14680064 | tf_op jit(solution)/shard_map/all_to_all | solution.py:51
  250.1 3.0 %copy.8 = bf16[1,128,28672]{2,1,0:T(8,128)(2,1)} copy(bf16[1,128,28672]{2,1,0:T(8,128)(2,1)S(1)} %bitcast.49) | data formatting | bytes 14680064
Async XLA Ops:
  0.7 28.2 %copy-start = (f32[1,16,28672]{2,1,0:T(8,128)S(1)}, f32[1,16,28672]{2,1,0:T(8,128)}, u32[]{:S(2)}) copy-start(f32[1,16,28672]{2,1,0:T(8,128)} %param.6) | copy-start | bytes 5505028
  0.7 28.2 %copy-start.1 = (f32[1,16,28672]{2,1,0:T(8,128)S(1)}, f32[1,16,28672]{2,1,0:T(8,128)}, u32[]{:S(2)}) copy-start(f32[1,16,28672]{2,1,0:T(8,128)} %param.7) | copy-start | bytes 5505028
  0.7 28.2 %copy-start.2 = (bf16[4,1,16,28672]{3,2,1,0:T(8,128)(2,1)S(1)}, bf16[4,1,16,28672]{3,2,1,0:T(8,128)(2,1)}, u32[]{:S(2)}) copy-start(bf16[4,1,16,28672]{3,2,1,0:T(8,128)(2,1)} %param.8) | copy-start | bytes 11010052
  5.3 23.5 %collective-permute-start = (f32[1,16,28672]{2,1,0:T(8,128)S(1)}, f32[1,16,28672]{2,1,0:T(8,128)S(1)}, u32[]{:S(2)}, u32[]{:S(2)}) collective-permute-start(f32[1,16,28672]{2,1,0:T(8,128)S(1)} %subtract_multiply_fusion.2), channel_id=1, source_target_pairs={{0,8},{8,16},{16,24},{24,32},{32,40},{40,48},{48,56},{56,64},{64,7... | collective-permute-start | bytes 5505032 | tf_op jit(solution)/shard_map/ppermute | solution.py:18
  5.3 22.8 %collective-permute-start.1 = (f32[1]{0:T(128)}, f32[1]{0:T(128)}, u32[]{:S(2)}, u32[]{:S(2)}) collective-permute-start(f32[1]{0:T(128)} %param.9), channel_id=1, source_target_pairs={{0,8},{8,16},{16,24},{24,32},{32,40},{40,48},{48,56},{56,64},{64,7... | collective-permute-start | bytes 20 | tf_op jit(solution)/shard_map/ppermute | solution.py:18
  31.1 42.1 %collective-permute-start.2 = (f32[1,16,28672]{2,1,0:T(8,128)S(1)}, f32[1,16,28672]{2,1,0:T(8,128)S(1)}, u32[]{:S(2)}, u32[]{:S(2)}) collective-permute-start(f32[1,16,28672]{2,1,0:T(8,128)S(1)} %subtract_multiply_fusion.1), channel_id=1, source_target_pairs={{0,16},{8,24},{16,32},{24,40},{32,48},{40,56},{48,64},{56,72},{64,... | collective-permute-start | bytes 5505032 | tf_op jit(solution)/shard_map/ppermute | solution.py:18
  35.1 37.5 %collective-permute-start.3 = (f32[1]{0:T(128)}, f32[1]{0:T(128)}, u32[]{:S(2)}, u32[]{:S(2)}) collective-permute-start(f32[1]{0:T(128)} %add.83), channel_id=1, source_target_pairs={{0,16},{8,24},{16,32},{24,40},{32,48},{40,56},{48,64},{56,72},{64,... | collective-permute-start | bytes 20 | tf_op jit(solution)/shard_map/ppermute | solution.py:18
  75.9 42.5 %collective-permute-start.4 = (f32[1,16,28672]{2,1,0:T(8,128)S(1)}, f32[1,16,28672]{2,1,0:T(8,128)S(1)}, u32[]{:S(2)}, u32[]{:S(2)}) collective-permute-start(f32[1,16,28672]{2,1,0:T(8,128)S(1)} %subtract_multiply_fusion), channel_id=1, source_target_pairs={{0,32},{8,40},{16,48},{24,56},{32,64},{40,72},{48,80},{56,88},{64,... | collective-permute-start | bytes 5505032 | tf_op jit(solution)/shard_map/ppermute | solution.py:18
  78.4 39.4 %collective-permute-start.5 = (f32[1]{0:T(128)}, f32[1]{0:T(128)}, u32[]{:S(2)}, u32[]{:S(2)}) collective-permute-start(f32[1]{0:T(128)} %add.89), channel_id=1, source_target_pairs={{0,32},{8,40},{16,48},{24,56},{32,64},{40,72},{48,80},{56,88},{64,... | collective-permute-start | bytes 20 | tf_op jit(solution)/shard_map/ppermute | solution.py:18
  121.6 40.0 %collective-permute-start.6 = (f32[1,16,28672]{2,1,0:T(8,128)S(1)}, f32[1,16,28672]{2,1,0:T(8,128)S(1)}, u32[]{:S(2)}, u32[]{:S(2)}) collective-permute-start(f32[1,16,28672]{2,1,0:T(8,128)S(1)} %fusion.12), channel_id=1, source_target_pairs={{0,64},{8,72},{16,80},{24,88},{32,96},{40,104},{48,112},{56,120},{... | collective-permute-start | bytes 5505032 | tf_op jit(solution)/shard_map/ppermute | solution.py:18
  121.7 39.2 %collective-permute-start.7 = (f32[1]{0:T(128)}, f32[1]{0:T(128)}, u32[]{:S(2)}, u32[]{:S(2)}) collective-permute-start(f32[1]{0:T(128)} %add.95), channel_id=1, source_target_pairs={{0,64},{8,72},{16,80},{24,88},{32,96},{40,104},{48,112},{56,120},{... | collective-permute-start | bytes 20 | tf_op jit(solution)/shard_map/ppermute | solution.py:18
